TPU v7x, 32 devices: a whole 2x2x4 slice. The times are simulated.
32 devices in a mesh: sub: 16 (over z, x, core), grid: 2 (over y).
Axes of the slice: x: 2, y: 2, z: 4, core: 2. Of those that a mesh axis runs over, the one named last changes fastest.
Arguments:
- front_entries: float32 [16, 12, 128, 2, 1536], P('sub', None, None, 'grid'), as said below
- coupling_rows: bfloat16 [16, 2048, 256], P('sub', 'grid'), may hold values from -0.09375 to 0.09375
- child_map: int32 [16, 2048], P('sub'), may hold values from 0 to 3071, as said below
Outputs:
- factored: float32 [16, 12, 128, 2, 1536], P('sub', None, None, 'grid')
Inputs may be any that keep to these rules, and one draw needn't show every extreme that they name: `child_map`: rows 2 p and 2 p + 1 each hold 2048 distinct indices, and together they name every index of the parent front. `front_entries`: each front is symmetric, and stays positive definite after both children's updates are subtracted.
All inputs are finite; a program needn't handle non-finite values.
Results may differ from a plain program's by a relative error of at most 0.0003.
Values may be sent and summed in bfloat16 or wider, within the bound.
A program may use at most 128 MiB of HBM per device.

v0:
```python
import jax
import jax.numpy as jnp
from jax import lax
from jax.sharding import PartitionSpec as P

NB = 128
PF = 3072
PIV = 1024


def partner(shard, axis, apart):
    return lax.ppermute(shard, axis, [(i, i ^ 1 << apart) for i in range(lax.axis_size(axis))])


def broadcast(shard, axis, root):
    mine = lax.axis_index(axis) == root
    return lax.psum(jnp.where(mine, shard, jnp.zeros_like(shard)), axis)


def invert_map(mapping):
    return (
        jnp.full((PF,), -1, jnp.int32)
        .at[mapping]
        .set(jnp.arange(mapping.shape[0], dtype=jnp.int32))
    )


def select_rows(table, inverse, wanted):
    index = inverse[wanted]
    found = index >= 0
    picked = table[jnp.where(found, index, 0)]
    return jnp.where(found[:, None], picked, jnp.zeros((), table.dtype))


def outer_product(left, right, precision):
    return lax.dot_general(
        left,
        right,
        (((1,), (1,)), ((), ())),
        precision=precision,
        preferred_element_type=jnp.float32,
    )


def block_indices(block_ids):
    offsets = jnp.arange(NB, dtype=jnp.int32)
    return (block_ids[:, None] * NB + offsets[None, :]).reshape(-1)


def on_device(front_entries, coupling_rows, child_map):
    sibling = lax.axis_index("sub") % 2
    column_owner = lax.axis_index("grid")
    grid_count = lax.axis_size("grid")
    row_blocks = front_entries.shape[1]
    col_width = front_entries.shape[4]
    col_blocks = col_width // NB
    local = front_entries.reshape(row_blocks * NB, col_width)
    row_block_ids = jnp.arange(row_blocks, dtype=jnp.int32) * 2 + sibling
    col_block_ids = jnp.arange(col_blocks, dtype=jnp.int32) * grid_count + column_owner
    my_rows = block_indices(row_block_ids)
    my_cols = block_indices(col_block_ids)
    own_map = child_map[0]
    own_inverse = invert_map(own_map)
    everything = lax.all_gather(coupling_rows, "grid", axis=1, tiled=True)[0]
    update = outer_product(coupling_rows[0], everything, None)
    dest_blocks = (
        jnp.arange(grid_count, dtype=jnp.int32)[:, None]
        + jnp.arange(col_blocks, dtype=jnp.int32)[None, :] * grid_count
    )
    dest_cols = block_indices(dest_blocks.reshape(-1))
    col_index = own_inverse[dest_cols]
    found = col_index >= 0
    spread = jnp.where(found[None, :], update[:, jnp.where(found, col_index, 0)], 0.0)
    spread = spread.reshape(update.shape[0], grid_count, col_width)
    arrived = (
        lax.all_to_all(spread.astype(jnp.bfloat16), "grid", split_axis=1, concat_axis=0, tiled=True)
        .astype(spread.dtype)
        .reshape(-1, col_width)
    )
    partner_rows = block_indices(jnp.arange(row_blocks, dtype=jnp.int32) * 2 + (1 - sibling))
    keep = select_rows(arrived, own_inverse, my_rows)
    give = select_rows(arrived, own_inverse, partner_rows)
    received = partner(give.astype(jnp.bfloat16), "sub", 0).astype(give.dtype)
    local = local - keep - received
    highest = lax.Precision.HIGHEST
    identity = jnp.eye(NB, dtype=jnp.float32)
    col_repeat = jnp.repeat(col_block_ids, NB)
    row_repeat = jnp.repeat(row_block_ids, NB)
    for step in range(PIV // NB):
        owner = step % grid_count
        local_col = step // grid_count * NB
        first = step // 2 * NB
        column = broadcast(local[:, local_col : local_col + NB], "grid", owner)
        own_pivot = local[first : first + NB, :]
        own_diag = column[first : first + NB]
        other_pivot, other_diag = (
            partner(own_pivot.astype(jnp.bfloat16), "sub", 0).astype(own_pivot.dtype),
            partner(own_diag.astype(jnp.bfloat16), "sub", 0).astype(own_diag.dtype),
        )
        holder = sibling == step % 2
        pivot_rows = jnp.where(holder, own_pivot, other_pivot)
        diagonal = jnp.where(holder, own_diag, other_diag)
        factor = jnp.linalg.cholesky(diagonal)
        inverse = jax.scipy.linalg.solve_triangular(factor, identity, lower=True)
        left = outer_product(column, inverse, highest)
        right = lax.dot_general(
            pivot_rows,
            inverse,
            (((0,), (1,)), ((), ())),
            precision=highest,
            preferred_element_type=jnp.float32,
        )
        left_live = jnp.where((row_repeat > step)[:, None], left, 0.0)
        right_live = jnp.where((col_repeat > step)[:, None], right, 0.0)
        local = local - outer_product(left_live, right_live, highest)
        is_owner = column_owner == owner
        current = local[:, local_col : local_col + NB]
        new_col = jnp.where(is_owner, jnp.where((row_repeat >= step)[:, None], left, 0.0), current)
        local = lax.dynamic_update_slice(local, new_col, (0, local_col))
    rows_global = my_rows[:, None]
    cols_global = my_cols[None, :]
    cleared = (cols_global < PIV) & (rows_global < cols_global) | (rows_global < PIV) & (
        cols_global >= PIV
    )
    result = jnp.where(cleared, 0.0, local)
    return result.reshape(front_entries.shape)


def solution(mesh):
    return jax.shard_map(
        on_device,
        mesh=mesh,
        in_specs=(P("sub", None, None, "grid", None), P("sub", "grid", None), P("sub", None)),
        out_specs=P("sub", None, None, "grid", None),
        check_vma=False,
    )
```

profile of v0, /device:TPU:0, one launch (start us, length us, event | category | flops | bytes accessed | tf_op | source)
XLA Modules:
  0.0 928.3 jit_solution(12365081881427203168)
XLA Ops:
  8.2 8.1 scatter_custom_fusion
  16.3 17.4 %gather_fusion.1 = s32[3072]{0:T(1024)S(1)} fusion(s32[3072]{0:T(1024)S(1)} %scatter_custom_fusion, s32[3072]{0:T(1024)S(1)} %broadcast_clamp_fusion.1), kind=kCustom, calls=%fused_computation.1 | custom fusion | bytes 36864 | tf_op jit(solution)/shard_map/gather | solution.py:71
  33.8 4.4 fusion
  38.2 18.6 %gather_fusion.2 = bf16[3072,1024]{1,0:T(8,128)(2,1)} fusion(bf16[1024,2048]{0,1:T(8,128)(2,1)} %fusion, s32[3072]{0:T(1024)S(1)} %broadcast_clamp_fusion), kind=kCustom, calls=%fused_computation.2 | custom fusion | bytes 12595200 | tf_op jit(solution)/shard_map/gather | solution.py:73
  56.8 6.9 select_convert_fusion
  63.7 6.3 all-to-all-start
  70.5 8.4 gather_fusion.4
  79.0 62.5 %all-to-all-done = bf16[1024,2,1536]{0,2,1:T(8,128)(2,1)} async-done(((bf16[1024,2,1536]{0,2,1:T(8,128)(2,1)}), bf16[1024,2,1536]{0,2,1:T(8,128)(2,1)}, u32[]{:S(2)}, u32[]{:S(2)}) %all-to-all-start) | async-done | bytes 6291488 | tf_op jit(solution)/shard_map/all_to_all | solution.py:76
  141.5 8.8 convert_bitcast_fusion
  150.3 12.6 %copy.43 = f32[2,1024,1,1536]{3,1,0,2:T(8,128)} copy(f32[2,1024,1,1536]{1,3,0,2:T(8,128)} %convert_bitcast_fusion) | data formatting | bytes 25165824 | tf_op jit(solution)/shard_map/convert_element_type | solution.py:77
  162.9 14.9 %gather_fusion.5 = bf16[1536,1536]{1,0:T(8,128)(2,1)} fusion(f32[2048,1536]{1,0:T(8,128)} %bitcast.198, s32[2048]{0:T(1024)S(1)} %pad_clamp_fusion), kind=kCustom, calls=%fused_computation.5 | custom fusion | bytes 9443328 | tf_op jit(solution)/shard_map/gather | solution.py:31
  177.8 6.6 copy.46
  184.4 5.4 select_convert_fusion.1
  190.6 8.4 gather_fusion
  199.0 8.9 copy.98
  207.9 9.6 %copy.45 = f32[1536,1536]{0,1:T(8,128)} copy(f32[1536,1536]{1,0:T(8,128)} %bitcast.201) | data formatting | bytes 18874368 | tf_op jit(solution)/shard_map/reshape | solution.py:57
  217.7 14.9 %gather_fusion.3 = f32[1536,1536]{1,0:T(8,128)} fusion(f32[2048,1536]{1,0:T(8,128)} %bitcast.199, s32[2048]{0:T(1024)S(1)} %pad_clamp_fusion.2), kind=kCustom, calls=%fused_computation.3 | custom fusion | bytes 18880512 | tf_op jit(solution)/shard_map/gather | solution.py:31
  232.6 9.6 %copy.44 = f32[1536,1536]{0,1:T(8,128)} copy(f32[1536,1536]{1,0:T(8,128)} %gather_fusion.3) | data formatting | bytes 18874368 | tf_op jit(solution)/shard_map/gather | solution.py:31
  242.3 8.6 convert_subtract_fusion
  250.9 3.7 copy-done.3
  256.4 34.3 %all-reduce.9.cloned.1.call-done = f32[1536,128]{0,1:T(8,128)} async-done(((f32[1536,128]{0,1:T(8,128)}), f32[1536,128]{0,1:T(8,128)}) %all-reduce.9.cloned.1.call-update) | async-done | bytes 786448 | tf_op jit(solution)/shard_map/psum | solution.py:17
  294.3 11.7 %cholesky.134 = f32[128,128]{1,0:T(8,128)S(1)} custom-call(f32[128,128]{1,0:T(8,128)S(1)} %fusion.106), custom_call_target="Cholesky" | custom-call | tf_op jit(solution)/shard_map/jit(cholesky)/cholesky | solution.py:103
  307.4 9.8 %custom-call.12 = f32[1,128,128]{1,2,0:T(8,128)S(1)} custom-call(f32[1,128,128]{2,1,0:T(8,128)S(1)} %fusion.83), custom_call_target="InvertDiagBlocksLowerTriangular" | custom-call | tf_op jit(solution)/shard_map/jit(_solve_triangular)/triangular_solve | solution.py:104
  321.6 11.9 %convolution_subtract_fusion.7 = f32[1536,1536]{0,1:T(8,128)} fusion(f32[1536,1536]{0,1:T(8,128)} %copy-done.3, f32[1536,128]{0,1:T(8,128)S(1)} %convolution_select_fusion.7, f32[1536,128]{0,1:T(8,128)S(1)} %fusion.125, pred[1536]{0:T(1024)(128)(4,1)S(1)} %broadcast_bitcast_fusion.23), kind=kOutput, calls=%fused_computation.16 | convolution fusion | flops 3626434560 | bytes 20448768 | tf_op jit(solution)/shard_map/dot_general | solution.py:36
  333.5 2.5 broadcast_select_fusion.3
  336.5 34.1 %all-reduce.11.cloned.1.call-done = f32[1536,128]{0,1:T(8,128)} async-done(((f32[1536,128]{0,1:T(8,128)}), f32[1536,128]{0,1:T(8,128)}) %all-reduce.11.cloned.1.call-update) | async-done | bytes 786448 | tf_op jit(solution)/shard_map/psum | solution.py:17
  374.1 11.7 %cholesky.145 = f32[128,128]{1,0:T(8,128)S(1)} custom-call(f32[128,128]{1,0:T(8,128)S(1)} %fusion.104), custom_call_target="Cholesky" | custom-call | tf_op jit(solution)/shard_map/jit(cholesky)/cholesky | solution.py:103
  387.2 9.8 %custom-call.13 = f32[1,128,128]{1,2,0:T(8,128)S(1)} custom-call(f32[1,128,128]{2,1,0:T(8,128)S(1)} %fusion.84), custom_call_target="InvertDiagBlocksLowerTriangular" | custom-call | tf_op jit(solution)/shard_map/jit(_solve_triangular)/triangular_solve | solution.py:104
  399.3 2.0 convolution_select_fusion.6
  401.4 10.6 %convolution_subtract_fusion.6 = f32[1536,1536]{0,1:T(8,128)S(1)} fusion(f32[1536,1536]{0,1:T(8,128)} %get-tuple-element.14, f32[1536,128]{0,1:T(8,128)S(1)} %convolution_select_fusion.6, f32[1536,128]{0,1:T(8,128)S(1)} %fusion.126, pred[1536]{0:T(1024)(128)(4,1)S(1)} %broadcast_bitcast_fusion.20), kind=kOutput, calls=%fused_computation.15 | convolution fusion | flops 3626434560 | bytes 20448768 | tf_op jit(solution)/shard_map/dot_general | solution.py:36
  412.2 3.7 copy-done
  417.6 33.8 %all-reduce.13.cloned.1.call-done = f32[1536,128]{0,1:T(8,128)} async-done(((f32[1536,128]{0,1:T(8,128)}), f32[1536,128]{0,1:T(8,128)}) %all-reduce.13.cloned.1.call-update) | async-done | bytes 786448 | tf_op jit(solution)/shard_map/psum | solution.py:17
  455.0 11.7 %cholesky.156 = f32[128,128]{1,0:T(8,128)S(1)} custom-call(f32[128,128]{1,0:T(8,128)S(1)} %fusion.102), custom_call_target="Cholesky" | custom-call | tf_op jit(solution)/shard_map/jit(cholesky)/cholesky | solution.py:103
  468.1 9.8 %custom-call.14 = f32[1,128,128]{1,2,0:T(8,128)S(1)} custom-call(f32[1,128,128]{2,1,0:T(8,128)S(1)} %fusion.85), custom_call_target="InvertDiagBlocksLowerTriangular" | custom-call | tf_op jit(solution)/shard_map/jit(_solve_triangular)/triangular_solve | solution.py:104
  482.3 11.9 %convolution_subtract_fusion.5 = f32[1536,1536]{0,1:T(8,128)} fusion(f32[1536,1536]{0,1:T(8,128)} %copy-done, f32[1536,128]{0,1:T(8,128)S(1)} %convolution_select_fusion.5, f32[1536,128]{0,1:T(8,128)S(1)} %fusion.127, pred[1536]{0:T(1024)(128)(4,1)S(1)} %broadcast_bitcast_fusion.17), kind=kOutput, calls=%fused_computation.14 | convolution fusion | flops 3626434560 | bytes 20448768 | tf_op jit(solution)/shard_map/dot_general | solution.py:36
  494.2 2.5 broadcast_select_fusion.2
  497.1 34.1 %all-reduce.15.cloned.1.call-done = f32[1536,128]{0,1:T(8,128)} async-done(((f32[1536,128]{0,1:T(8,128)}), f32[1536,128]{0,1:T(8,128)}) %all-reduce.15.cloned.1.call-update) | async-done | bytes 786448 | tf_op jit(solution)/shard_map/psum | solution.py:17
  534.8 11.7 %cholesky.167 = f32[128,128]{1,0:T(8,128)S(1)} custom-call(f32[128,128]{1,0:T(8,128)S(1)} %fusion.100), custom_call_target="Cholesky" | custom-call | tf_op jit(solution)/shard_map/jit(cholesky)/cholesky | solution.py:103
  547.9 9.8 %custom-call.15 = f32[1,128,128]{1,2,0:T(8,128)S(1)} custom-call(f32[1,128,128]{2,1,0:T(8,128)S(1)} %fusion.86), custom_call_target="InvertDiagBlocksLowerTriangular" | custom-call | tf_op jit(solution)/shard_map/jit(_solve_triangular)/triangular_solve | solution.py:104
  562.1 10.6 %convolution_subtract_fusion.4 = f32[1536,1536]{0,1:T(8,128)S(1)} fusion(f32[1536,1536]{0,1:T(8,128)} %get-tuple-element.12, f32[1536,128]{0,1:T(8,128)S(1)} %convolution_select_fusion.4, f32[1536,128]{0,1:T(8,128)S(1)} %fusion.128, pred[1536]{0:T(1024)(128)(4,1)S(1)} %broadcast_bitcast_fusion.14), kind=kOutput, calls=%fused_computation.13 | convolution fusion | flops 3626434560 | bytes 20448768 | tf_op jit(solution)/shard_map/dot_general | solution.py:36
  572.9 3.7 copy-done.1
  578.3 33.8 %all-reduce.17.cloned.1.call-done = f32[1536,128]{0,1:T(8,128)} async-done(((f32[1536,128]{0,1:T(8,128)}), f32[1536,128]{0,1:T(8,128)}) %all-reduce.17.cloned.1.call-update) | async-done | bytes 786448 | tf_op jit(solution)/shard_map/psum | solution.py:17
  615.7 11.7 %cholesky.178 = f32[128,128]{1,0:T(8,128)S(1)} custom-call(f32[128,128]{1,0:T(8,128)S(1)} %fusion.98), custom_call_target="Cholesky" | custom-call | tf_op jit(solution)/shard_map/jit(cholesky)/cholesky | solution.py:103
  628.8 9.8 %custom-call.16 = f32[1,128,128]{1,2,0:T(8,128)S(1)} custom-call(f32[1,128,128]{2,1,0:T(8,128)S(1)} %fusion.87), custom_call_target="InvertDiagBlocksLowerTriangular" | custom-call | tf_op jit(solution)/shard_map/jit(_solve_triangular)/triangular_solve | solution.py:104
  642.9 11.9 %convolution_subtract_fusion.3 = f32[1536,1536]{0,1:T(8,128)} fusion(f32[1536,1536]{0,1:T(8,128)} %copy-done.1, f32[1536,128]{0,1:T(8,128)S(1)} %convolution_select_fusion.3, f32[1536,128]{0,1:T(8,128)S(1)} %fusion.129, pred[1536]{0:T(1024)(128)(4,1)S(1)} %broadcast_bitcast_fusion.11), kind=kOutput, calls=%fused_computation.12 | convolution fusion | flops 3626434560 | bytes 20448768 | tf_op jit(solution)/shard_map/dot_general | solution.py:36
  654.8 2.5 broadcast_select_fusion.1
  657.8 34.1 %all-reduce.19.cloned.1.call-done = f32[1536,128]{0,1:T(8,128)} async-done(((f32[1536,128]{0,1:T(8,128)}), f32[1536,128]{0,1:T(8,128)}) %all-reduce.19.cloned.1.call-update) | async-done | bytes 786448 | tf_op jit(solution)/shard_map/psum | solution.py:17
  695.5 11.7 %cholesky.189 = f32[128,128]{1,0:T(8,128)S(1)} custom-call(f32[128,128]{1,0:T(8,128)S(1)} %fusion.96), custom_call_target="Cholesky" | custom-call | tf_op jit(solution)/shard_map/jit(cholesky)/cholesky | solution.py:103
  708.6 9.8 %custom-call.17 = f32[1,128,128]{1,2,0:T(8,128)S(1)} custom-call(f32[1,128,128]{2,1,0:T(8,128)S(1)} %fusion.88), custom_call_target="InvertDiagBlocksLowerTriangular" | custom-call | tf_op jit(solution)/shard_map/jit(_solve_triangular)/triangular_solve | solution.py:104
  722.7 10.6 %convolution_subtract_fusion.2 = f32[1536,1536]{0,1:T(8,128)S(1)} fusion(f32[1536,1536]{0,1:T(8,128)} %get-tuple-element.10, f32[1536,128]{0,1:T(8,128)S(1)} %convolution_select_fusion.2, f32[1536,128]{0,1:T(8,128)S(1)} %fusion.130, pred[1536]{0:T(1024)(128)(4,1)S(1)} %broadcast_bitcast_fusion.8), kind=kOutput, calls=%fused_computation.11 | convolution fusion | flops 3626434560 | bytes 20448768 | tf_op jit(solution)/shard_map/dot_general | solution.py:36
  733.5 3.7 copy-done.2
  738.8 34.0 %all-reduce.21.cloned.1.call-done = f32[1536,128]{0,1:T(8,128)} async-done(((f32[1536,128]{0,1:T(8,128)}), f32[1536,128]{0,1:T(8,128)}) %all-reduce.21.cloned.1.call-update) | async-done | bytes 786448 | tf_op jit(solution)/shard_map/psum | solution.py:17
  776.4 11.7 %cholesky.200 = f32[128,128]{1,0:T(8,128)S(1)} custom-call(f32[128,128]{1,0:T(8,128)S(1)} %fusion.94), custom_call_target="Cholesky" | custom-call | tf_op jit(solution)/shard_map/jit(cholesky)/cholesky | solution.py:103
  789.5 9.8 %custom-call.18 = f32[1,128,128]{1,2,0:T(8,128)S(1)} custom-call(f32[1,128,128]{2,1,0:T(8,128)S(1)} %fusion.89), custom_call_target="InvertDiagBlocksLowerTriangular" | custom-call | tf_op jit(solution)/shard_map/jit(_solve_triangular)/triangular_solve | solution.py:104
  803.6 12.3 %convolution_subtract_fusion.1 = f32[1536,1536]{0,1:T(8,128)} fusion(f32[1536,1536]{0,1:T(8,128)} %copy-done.2, f32[1536,128]{0,1:T(8,128)S(1)} %convolution_select_fusion.1, f32[1536,128]{0,1:T(8,128)S(1)} %fusion.131, pred[1536]{0:T(1024)(128)(4,1)S(1)} %broadcast_bitcast_fusion.5), kind=kOutput, calls=%fused_computation.10 | convolution fusion | flops 3626434560 | bytes 20448768 | tf_op jit(solution)/shard_map/dot_general | solution.py:36
  815.9 2.5 broadcast_select_fusion
  818.7 34.3 %all-reduce.23.cloned.1.call-done = f32[1536,128]{0,1:T(8,128)} async-done(((f32[1536,128]{0,1:T(8,128)}), f32[1536,128]{0,1:T(8,128)}) %all-reduce.23.cloned.1.call-update) | async-done | bytes 786448 | tf_op jit(solution)/shard_map/psum | solution.py:17
  856.6 11.7 %cholesky.211 = f32[128,128]{1,0:T(8,128)S(1)} custom-call(f32[128,128]{1,0:T(8,128)S(1)} %fusion.92), custom_call_target="Cholesky" | custom-call | tf_op jit(solution)/shard_map/jit(cholesky)/cholesky | solution.py:103
  869.7 9.8 %custom-call.19 = f32[1,128,128]{1,2,0:T(8,128)S(1)} custom-call(f32[1,128,128]{2,1,0:T(8,128)S(1)} %fusion.90), custom_call_target="InvertDiagBlocksLowerTriangular" | custom-call | tf_op jit(solution)/shard_map/jit(_solve_triangular)/triangular_solve | solution.py:104
  881.8 2.0 convolution_select_fusion
  883.8 10.8 %convolution_subtract_fusion = f32[1536,1536]{0,1:T(8,128)S(1)} fusion(f32[1536,1536]{0,1:T(8,128)} %get-tuple-element.8, f32[1536,128]{0,1:T(8,128)S(1)} %convolution_select_fusion, f32[1536,128]{0,1:T(8,128)S(1)} %fusion.132, pred[1536]{0:T(1024)(128)(4,1)S(1)} %broadcast_bitcast_fusion.2), kind=kOutput, calls=%fused_computation.9 | convolution fusion | flops 3626434560 | bytes 20448768 | tf_op jit(solution)/shard_map/dot_general | solution.py:36
  894.8 5.1 or_select_fusion
  899.9 9.6 %copy.79 = f32[1536,1536]{1,0:T(8,128)} copy(f32[1536,1536]{0,1:T(8,128)} %or_select_fusion) | data formatting | bytes 18874368 | tf_op jit(solution)/shard_map/jit(_where)/select_n | solution.py:125
  909.6 12.0 %copy.80 = f32[1,12,128,1,1536]{4,3,2,1,0:T(1,128)} copy(f32[1,12,128,1,1536]{4,2,1,3,0:T(8,128)} %bitcast.200) | data formatting | bytes 18874368 | tf_op jit(solution)/shard_map/reshape | solution.py:126
  (231 shorter events, 81.9 us)
Async XLA Ops:
  6.5 27.2 %copy-start.4 = (bf16[1,1024,256]{2,1,0:T(8,128)(2,1)S(1)}, bf16[1,1024,256]{2,1,0:T(8,128)(2,1)}, u32[]{:S(2)}) copy-start(bf16[1,1024,256]{2,1,0:T(8,128)(2,1)} %param.7) | copy-start | bytes 1572868
  6.5 27.2 %all-gather.2.cloned.1.call-start = ((), (), s32[]{:S(2)}) async-start(), calls=%async_computation.1 | async-start | bytes 1572864 | tf_op jit(solution)/shard_map/all_gather | solution.py:64
  63.7 77.7 %all-to-all-start = ((bf16[1024,2,1536]{0,2,1:T(8,128)(2,1)}), bf16[1024,2,1536]{0,2,1:T(8,128)(2,1)}, u32[]{:S(2)}, u32[]{:S(2)}) async-start(bf16[1024,2,1536]{0,2,1:T(8,128)(2,1)} %select_convert_fusion), calls=%async_computation | async-start | bytes 12582912 | tf_op jit(solution)/shard_map/all_to_all | solution.py:76
  70.0 220.7 %all-reduce.9.cloned.1.call-start = ((), (), s32[]{:S(2)}) async-start(), calls=%async_computation.2 | async-start | bytes 1572864 | tf_op jit(solution)/shard_map/psum | solution.py:17
  189.9 52.4 %collective-permute-start = (bf16[1536,1536]{0,1:T(8,128)(2,1)}, bf16[1536,1536]{0,1:T(8,128)(2,1)}, u32[]{:S(2)}, u32[]{:S(2)}) collective-permute-start(bf16[1536,1536]{0,1:T(8,128)(2,1)} %select_convert_fusion.1), channel_id=1, source_target_pairs={{0,2},{2,0},{4,6},{6,4},{8,10},{10,8},{12,14},{14,12},{16,18},{18,... | collective-permute-start | bytes 14155784 | tf_op jit(solution)/shard_map/ppermute | solution.py:12
  250.9 3.7 copy-start.3
  255.6 115.0 %all-reduce.11.cloned.1.call-start = ((), (), s32[]{:S(2)}) async-start(), calls=%async_computation.3 | async-start | bytes 1572864 | tf_op jit(solution)/shard_map/psum | solution.py:17
  291.6 1.8 collective-permute-start.1
  292.8 26.7 %collective-permute-start.2 = (bf16[128,1536]{0,1:T(8,128)(2,1)S(1)}, bf16[128,1536]{0,1:T(8,128)(2,1)S(1)}, u32[]{:S(2)}, u32[]{:S(2)}) collective-permute-start(bf16[128,1536]{0,1:T(8,128)(2,1)S(1)} %slice.263), channel_id=1, source_target_pairs={{0,2},{2,0},{4,6},{6,4},{8,10},{10,8},{12,14},{14,12},{16,18},{18,... | collective-permute-start | bytes 1179656 | tf_op jit(solution)/shard_map/ppermute | solution.py:12
  336.0 115.5 %all-reduce.13.cloned.1.call-start = ((), (), s32[]{:S(2)}) async-start(), calls=%async_computation.4 | async-start | bytes 1572864 | tf_op jit(solution)/shard_map/psum | solution.py:17
  371.4 1.8 collective-permute-start.3
  372.6 26.7 %collective-permute-start.4 = (bf16[128,1536]{0,1:T(8,128)(2,1)S(1)}, bf16[128,1536]{0,1:T(8,128)(2,1)S(1)}, u32[]{:S(2)}, u32[]{:S(2)}) collective-permute-start(bf16[128,1536]{0,1:T(8,128)(2,1)S(1)} %slice.262), channel_id=1, source_target_pairs={{0,2},{2,0},{4,6},{6,4},{8,10},{10,8},{12,14},{14,12},{16,18},{18,... | collective-permute-start | bytes 1179656 | tf_op jit(solution)/shard_map/ppermute | solution.py:12
  412.2 3.7 copy-start
  416.9 114.3 %all-reduce.15.cloned.1.call-start = ((), (), s32[]{:S(2)}) async-start(), calls=%async_computation.5 | async-start | bytes 1572864 | tf_op jit(solution)/shard_map/psum | solution.py:17
  452.3 1.8 collective-permute-start.5
  453.5 26.7 %collective-permute-start.6 = (bf16[128,1536]{0,1:T(8,128)(2,1)S(1)}, bf16[128,1536]{0,1:T(8,128)(2,1)S(1)}, u32[]{:S(2)}, u32[]{:S(2)}) collective-permute-start(bf16[128,1536]{0,1:T(8,128)(2,1)S(1)} %slice.261), channel_id=1, source_target_pairs={{0,2},{2,0},{4,6},{6,4},{8,10},{10,8},{12,14},{14,12},{16,18},{18,... | collective-permute-start | bytes 1179656 | tf_op jit(solution)/shard_map/ppermute | solution.py:12
  496.7 115.4 %all-reduce.17.cloned.1.call-start = ((), (), s32[]{:S(2)}) async-start(), calls=%async_computation.6 | async-start | bytes 1572864 | tf_op jit(solution)/shard_map/psum | solution.py:17
  532.1 1.8 collective-permute-start.7
  533.3 26.7 %collective-permute-start.8 = (bf16[128,1536]{0,1:T(8,128)(2,1)S(1)}, bf16[128,1536]{0,1:T(8,128)(2,1)S(1)}, u32[]{:S(2)}, u32[]{:S(2)}) collective-permute-start(bf16[128,1536]{0,1:T(8,128)(2,1)S(1)} %slice.260), channel_id=1, source_target_pairs={{0,2},{2,0},{4,6},{6,4},{8,10},{10,8},{12,14},{14,12},{16,18},{18,... | collective-permute-start | bytes 1179656 | tf_op jit(solution)/shard_map/ppermute | solution.py:12
  572.9 3.7 copy-start.1
  577.6 114.3 %all-reduce.19.cloned.1.call-start = ((), (), s32[]{:S(2)}) async-start(), calls=%async_computation.7 | async-start | bytes 1572864 | tf_op jit(solution)/shard_map/psum | solution.py:17
  613.0 1.8 collective-permute-start.9
  614.2 26.7 %collective-permute-start.10 = (bf16[128,1536]{0,1:T(8,128)(2,1)S(1)}, bf16[128,1536]{0,1:T(8,128)(2,1)S(1)}, u32[]{:S(2)}, u32[]{:S(2)}) collective-permute-start(bf16[128,1536]{0,1:T(8,128)(2,1)S(1)} %slice.259), channel_id=1, source_target_pairs={{0,2},{2,0},{4,6},{6,4},{8,10},{10,8},{12,14},{14,12},{16,18},{18,... | collective-permute-start | bytes 1179656 | tf_op jit(solution)/shard_map/ppermute | solution.py:12
  657.3 115.5 %all-reduce.21.cloned.1.call-start = ((), (), s32[]{:S(2)}) async-start(), calls=%async_computation.8 | async-start | bytes 1572864 | tf_op jit(solution)/shard_map/psum | solution.py:17
  692.8 1.8 collective-permute-start.11
  694.0 26.7 %collective-permute-start.12 = (bf16[128,1536]{0,1:T(8,128)(2,1)S(1)}, bf16[128,1536]{0,1:T(8,128)(2,1)S(1)}, u32[]{:S(2)}, u32[]{:S(2)}) collective-permute-start(bf16[128,1536]{0,1:T(8,128)(2,1)S(1)} %slice.258), channel_id=1, source_target_pairs={{0,2},{2,0},{4,6},{6,4},{8,10},{10,8},{12,14},{14,12},{16,18},{18,... | collective-permute-start | bytes 1179656 | tf_op jit(solution)/shard_map/ppermute | solution.py:12
  733.5 3.7 copy-start.2
  738.3 114.7 %all-reduce.23.cloned.1.call-start = ((), (), s32[]{:S(2)}) async-start(), calls=%async_computation.9 | async-start | bytes 1572864 | tf_op jit(solution)/shard_map/psum | solution.py:17
  773.6 1.8 collective-permute-start.13
  774.8 26.7 %collective-permute-start.14 = (bf16[128,1536]{0,1:T(8,128)(2,1)S(1)}, bf16[128,1536]{0,1:T(8,128)(2,1)S(1)}, u32[]{:S(2)}, u32[]{:S(2)}) collective-permute-start(bf16[128,1536]{0,1:T(8,128)(2,1)S(1)} %slice.257), channel_id=1, source_target_pairs={{0,2},{2,0},{4,6},{6,4},{8,10},{10,8},{12,14},{14,12},{16,18},{18,... | collective-permute-start | bytes 1179656 | tf_op jit(solution)/shard_map/ppermute | solution.py:12
  853.8 1.8 collective-permute-start.15
  855.0 26.7 %collective-permute-start.16 = (bf16[128,1536]{0,1:T(8,128)(2,1)S(1)}, bf16[128,1536]{0,1:T(8,128)(2,1)S(1)}, u32[]{:S(2)}, u32[]{:S(2)}) collective-permute-start(bf16[128,1536]{0,1:T(8,128)(2,1)S(1)} %slice.256), channel_id=1, source_target_pairs={{0,2},{2,0},{4,6},{6,4},{8,10},{10,8},{12,14},{14,12},{16,18},{18,... | collective-permute-start | bytes 1179656 | tf_op jit(solution)/shard_map/ppermute | solution.py:12
  883.8 11.0 %copy-start.5 = (s32[1536]{0:T(1024)S(1)}, s32[1536]{0:T(1024)}, u32[]{:S(2)}) copy-start(s32[1536]{0:T(1024)} %get-tuple-element.17) | copy-start | bytes 18436
Sparse Core Ops, SparseCore 0:
  8.9 23.9 all-gather.1
  255.7 34.9 all-reduce.8
  336.1 34.4 all-reduce.10
  417.0 34.3 all-reduce.12
  496.8 34.4 all-reduce.14
  577.7 34.3 all-reduce.16
  657.5 34.4 all-reduce.18
  738.4 34.3 all-reduce.20
  818.5 34.3 all-reduce.22
where the time goes:
time: 936 us; the launch traced here: 928 us
  waiting for transfers between devices  336 us (36%)
  other arithmetic  242 us (26%)
  local copies, waits for them, and re-layouts  193 us (21%)
  matrix products  129 us (14%)
  between operations  14.4 us (2%)
  starting transfers between devices  13.6 us (1%)
    psum x8, waiting for transfers between devices, broadcast(): return lax.psum(jnp.where(mine, shard, jnp.zeros_like(shard)), axis)  273 us
    dot_general x17, matrix products, outer_product(): lax.dot_general(left, right, (((1,), (1,)), ((), ())), precision=precisio...  111 us
    another operation x24, other arithmetic, on_device(): factor = jnp.linalg.cholesky(diagonal)  99.6 us
    another operation x16, other arithmetic, on_device(): inverse = jax.scipy.linalg.solve_triangular(factor, identity, lower=True)  83.6 us
    all_to_all x1, waiting for transfers between devices, on_device(): lax.all_to_all(spread.astype(jnp.bfloat16), 'grid', split_axis=1, concat_...  62.5 us
    gather x4, local copies, waits for them, and re-layouts, select_rows(): picked = table[jnp.where(found, index, 0)]  46.1 us
    unnamed x13, local copies, waits for them, and re-layouts  23.9 us
  transfers between devices with their start and end apart: 27, of which 9 were waited for; matrix products, arithmetic and copies ran while one was open for 33% of the time, Pallas kernels for 0%

commit v1 on v0

v1 whole, which is shorter than its diff:
```python
import functools

import jax
import jax.numpy as jnp
from jax import lax
from jax.experimental import pallas as pl
from jax.experimental.pallas import tpu as pltpu
from jax.sharding import PartitionSpec as P

NB = 128
PF = 3072
PIV = 1024
NPB = PIV // NB
SUBL = 8
EXTRA = 16
NT = (((1,), (1,)), ((), ()))
NN = (((1,), (0,)), ((), ()))
F32 = jnp.float32
BF16 = jnp.bfloat16


def dot(a, b, dims=NN):
    return lax.dot_general(a, b, dims, preferred_element_type=F32)


def split(x):
    high = x.astype(BF16)
    return high, (x - high.astype(F32)).astype(BF16)


def dot3(a, b, dims=NN):
    ah, al = split(a)
    bh, bl = split(b)
    return dot(ah, bh, dims) + (dot(al, bh, dims) + dot(ah, bl, dims))


def sibling_swap(shard):
    return lax.ppermute(shard, "sub", [(i, i ^ 1) for i in range(lax.axis_size("sub"))])


def ring_gather(shard):
    count = lax.axis_size("grid")
    parts = [shard]
    for k in range(1, count):
        parts.append(lax.ppermute(shard, "grid", [((i + k) % count, i) for i in range(count)]))
    return jnp.stack(parts)


def block(index):
    return pl.ds(pl.multiple_of(index * NB, NB), NB)


def expand_kernel(map_ref, rows_ref, out_ref):
    rows = out_ref.shape[0]
    width = rows_ref.shape[2]
    first = pl.program_id(0) * rows
    for child in range(2):
        ids = first + lax.broadcasted_iota(jnp.int32, (rows, map_ref.shape[2]), 0)
        hot = jnp.where(map_ref[child] == ids, 1.0, 0.0).astype(BF16)
        out_ref[:, child * width : (child + 1) * width] = dot(hot, rows_ref[child]).astype(BF16)


def expand(maps, rows):
    tile = 256
    width = rows.shape[2]
    return pl.pallas_call(
        expand_kernel,
        grid=(PF // tile,),
        in_specs=[
            pl.BlockSpec(maps.shape, lambda i: (0, 0, 0)),
            pl.BlockSpec(rows.shape, lambda i: (0, 0, 0)),
        ],
        out_specs=pl.BlockSpec((tile, 2 * width), lambda i: (i, 0)),
        out_shape=jax.ShapeDtypeStruct((PF, 2 * width), BF16),
        name="expand",
    )(maps, rows)


def factor_block(diag):
    groups = NB // SUBL
    a = [diag[v * SUBL : (v + 1) * SUBL] for v in range(groups)]
    lane = lax.broadcasted_iota(jnp.int32, (SUBL, NB), 1)
    sub = lax.broadcasted_iota(jnp.int32, (SUBL, NB), 0)

    def along(x, row):
        return jnp.broadcast_to(x[row : row + 1], (SUBL, NB))

    for t in range(groups):
        cols = [
            [jnp.broadcast_to(a[v][:, t * SUBL + l : t * SUBL + l + 1], (SUBL, NB)) for l in range(SUBL)]
            for v in range(t, groups)
        ]
        for l in range(SUBL):
            inv_pivot = 1.0 / along(cols[0][l], l)
            row = along(a[t], l) * jnp.where(lane == t * SUBL + l, 2.0, 1.0)
            ahead = [along(cols[0][k], l) for k in range(l + 1, SUBL)]
            for v in range(t, groups):
                mine = cols[v - t]
                m = mine[l] * inv_pivot
                if v == t:
                    m = jnp.where(sub > l, m, 0.0)
                a[v] = a[v] - m * row
                for k in range(l + 1, SUBL):
                    mine[k] = mine[k] - m * ahead[k - l - 1]
    d_lane = jnp.zeros((SUBL, NB), F32)
    on_diag = []
    for v in range(groups):
        on_diag.append(jnp.where(lane == v * SUBL + sub, a[v], 0.0))
        d_lane = d_lane + on_diag[v]
    inv_lane = 1.0 / jnp.sum(d_lane, axis=0, keepdims=True)
    inverse, upper = [], []
    for v in range(groups):
        scale = 1.0 / jnp.sqrt(jnp.sum(on_diag[v], axis=1, keepdims=True))
        at = v * SUBL + sub
        inverse.append(jnp.where(lane <= at, a[v] * inv_lane * scale, 0.0))
        upper.append(jnp.where(lane >= at, a[v] * scale, 0.0))
    return jnp.concatenate(inverse, 0), jnp.concatenate(upper, 0)


def pivot_kernel(grid_count, me_ref, front_ref, rows_ref, factor_ref, high_ref, low_ref, w):
    s, g = me_ref[0], me_ref[1]
    held = front_ref.shape[2] - EXTRA
    eye = lax.broadcasted_iota(jnp.int32, (NB, NB), 0) == lax.broadcasted_iota(jnp.int32, (NB, NB), 1)
    for i in range(NPB):
        at = slice(i * NB, (i + 1) * NB)
        w[at, :] = -dot(rows_ref[at, :], rows_ref[...], NT)
        from_row = lax.rem(i + s, 2)
        for b in range(NPB):
            k = lax.rem(b - g + PIV // NB * grid_count, grid_count)
            cols = slice(b // grid_count * NB, (b // grid_count + 1) * NB)
            there = slice(b * NB, (b + 1) * NB)
            piece = front_ref[from_row, k, i // 2 * NB : (i // 2 + 1) * NB, cols].astype(F32)
            if b == i:
                rest = front_ref[from_row, k, held : held + EXTRA, cols].astype(F32)[:1]
                piece = piece + jnp.where(eye, rest, 0.0)
            w[at, there] += piece

    @pl.loop(0, NPB)
    def _(j):
        at = block(j)
        inverse, upper = factor_block(w[at, at])
        factor_ref[at, at] = upper.T
        w[at, at] = jnp.where(eye, 1.0, 0.0)
        panel = dot3(inverse, w[at, :])
        w[at, :] = panel
        panel16 = panel.astype(BF16)

        @pl.loop(j + 1, NPB)
        def _(i):
            mine = block(i)
            left = w[at, mine].T
            factor_ref[mine, at] = left
            w[mine, at] = jnp.zeros((NB, NB), F32)
            w[mine, :] -= dot(left.astype(BF16), panel16)

    for i in range(NPB):
        at = slice(i * NB, (i + 1) * NB)
        keep = lax.broadcasted_iota(jnp.int32, (NB, PIV), 1) < (i + 1) * NB
        high, low = split(jnp.where(keep, w[at, :], 0.0))
        high_ref[at, :] = high
        low_ref[at, :] = low


def factor_pivots(me, fronts, expanded, grid_count):
    vmem = pl.BlockSpec(memory_space=pltpu.VMEM)
    square = functools.partial(jax.ShapeDtypeStruct, (PIV, PIV))
    return pl.pallas_call(
        functools.partial(pivot_kernel, grid_count),
        grid=(1,),
        in_specs=[
            pl.BlockSpec(memory_space=pltpu.SMEM),
            vmem,
            pl.BlockSpec((PIV, expanded.shape[1]), lambda i: (0, 0)),
        ],
        out_specs=[vmem, vmem, vmem],
        out_shape=[square(F32), square(BF16), square(BF16)],
        scratch_shapes=[pltpu.VMEM((PIV, PIV), F32)],
        cost_estimate=pl.CostEstimate(flops=40 * PIV**3, bytes_accessed=16 * PIV**2, transcendentals=0),
        name="pivots",
    )(me, fronts, expanded)


def schur_kernel(
    grid_count, me_ref, front_ref, left_ref, right_ref, rows_ref, factor_ref, high_ref, low_ref,
    out_ref, mycols, across, xr, xl,
):
    s, g = me_ref[0], me_ref[1]
    r = pl.program_id(0)
    col_blocks = out_ref.shape[0] // NB
    done = NPB // grid_count

    @pl.when(r == 0)
    def _():
        for c in range(col_blocks):
            mycols[c * NB : (c + 1) * NB, :] = rows_ref[block(c * grid_count + g), :]
        for i in range(NPB):
            at = slice(i * NB, (i + 1) * NB)
            piece = right_ref[lax.rem(i + s, 2), i // 2 * NB : (i // 2 + 1) * NB, :].astype(F32)
            across[at, :] = (piece - dot(rows_ref[at, :], mycols[done * NB :, :], NT)).astype(BF16)
        for i in range(NPB):
            at = slice(i * NB, (i + 1) * NB)
            deep = (i + 1) * NB
            xr[at, :] = dot(high_ref[at, :deep], across[:deep, :]).astype(BF16)

    row_id = 2 * r + s

    @pl.when(r < NPB // 2)
    def _():
        for c in range(col_blocks):
            to = pl.ds(c, NB, stride=col_blocks)
            if c < done:
                col_id = c * grid_count + g
                here = factor_ref[block(row_id), block(col_id)]
                out_ref[to, :] = jnp.where(row_id >= col_id, here, 0.0)
            else:
                out_ref[to, :] = jnp.zeros((NB, NB), F32)

    @pl.when(r >= NPB // 2)
    def _():
        mine = rows_ref[block(row_id), :]
        local = block(r - NPB // 2)
        for b in range(NPB):
            k = lax.rem(b - g + NPB * grid_count, grid_count)
            cols = slice(b // grid_count * NB, (b // grid_count + 1) * NB)
            xl[:, b * NB : (b + 1) * NB] = left_ref[k, local, cols].astype(F32)
        a_high, a_low = split(xl[...] - dot(mine, rows_ref[:PIV, :], NT))
        x = dot(a_high, high_ref[...], NT) + (dot(a_low, high_ref[...], NT) + dot(a_high, low_ref[...], NT))
        xl[...] = x
        x16 = x.astype(BF16)
        taken = dot(mine, mycols[done * NB :, :], NT) + dot(x16, xr[...])
        for c in range(col_blocks):
            to = pl.ds(c, NB, stride=col_blocks)
            if c < done:
                out_ref[to, :] = xl[:, block(c * grid_count + g)]
            else:
                out_ref[to, :] = front_ref[to, :] - taken[:, (c - done) * NB : (c - done + 1) * NB]


def schur(me, front, left, right, expanded, factor, high, low, grid_count, col_blocks):
    vmem = pl.BlockSpec(memory_space=pltpu.VMEM)
    tall = NB * col_blocks
    below = (col_blocks - NPB // grid_count) * NB
    return pl.pallas_call(
        functools.partial(schur_kernel, grid_count),
        grid=(front.shape[0] // tall,),
        in_specs=[
            pl.BlockSpec(memory_space=pltpu.SMEM),
            pl.BlockSpec((tall, NB), lambda i: (jnp.maximum(i, NPB // 2), 0)),
        ]
        + [vmem] * 6,
        out_specs=pl.BlockSpec((tall, NB), lambda i: (i, 0)),
        out_shape=jax.ShapeDtypeStruct(front.shape, F32),
        scratch_shapes=[
            pltpu.VMEM((col_blocks * NB, expanded.shape[1]), BF16),
            pltpu.VMEM((PIV, below), BF16),
            pltpu.VMEM((PIV, below), BF16),
            pltpu.VMEM((NB, PIV), F32),
        ],
        compiler_params=pltpu.CompilerParams(vmem_limit_bytes=56 * 1024 * 1024),
        name="schur",
    )(me, front, left, right, expanded, factor, high, low)


def on_device(front_entries, coupling_rows, child_map):
    s = lax.axis_index("sub") % 2
    g = lax.axis_index("grid")
    grid_count = lax.axis_size("grid")
    row_blocks = front_entries.shape[1]
    col_width = front_entries.shape[4]
    col_blocks = col_width // NB
    wide = front_entries.reshape(row_blocks * NB, col_width)
    front = front_entries.reshape(row_blocks * NB * col_blocks, NB)
    me = jnp.stack([s, g]).astype(jnp.int32)
    top, pivot_cols = PIV // 2, PIV // grid_count

    own_rows = ring_gather(coupling_rows[0]).reshape(-1, coupling_rows.shape[2])
    own_map = jnp.roll(child_map[0].reshape(grid_count, -1), -g, axis=0).reshape(1, -1)
    rows = jnp.stack([own_rows, sibling_swap(own_rows)])
    maps = jnp.stack([own_map, sibling_swap(own_map)])

    corner = wide[:top, :pivot_cols]
    rounded = lax.reduce_precision(corner, 8, 7)
    row_ids = (jnp.arange(top, dtype=jnp.int32) // NB * 2 + s) * NB + jnp.arange(top, dtype=jnp.int32) % NB
    spots = jnp.arange(pivot_cols, dtype=jnp.int32)
    col_ids = (spots // NB * grid_count + g) * NB + spots % NB
    rest = jnp.sum(jnp.where(row_ids[:, None] == col_ids[None, :], corner - rounded, 0.0), axis=0)
    piece = jnp.concatenate(
        [corner.astype(BF16), jnp.broadcast_to(rest.astype(BF16)[None], (EXTRA, pivot_cols))]
    )
    held = ring_gather(piece)
    pivots = jnp.stack([held, sibling_swap(held)])
    left = ring_gather(wide[top:, :pivot_cols].astype(BF16))
    over = wide[:top, pivot_cols:].astype(BF16)
    right = jnp.stack([over, sibling_swap(over)])

    expanded = expand(maps, rows)
    factor, high, low = factor_pivots(me, pivots, expanded, grid_count)
    result = schur(me, front, left, right, expanded, factor, high, low, grid_count, col_blocks)
    return result.reshape(front_entries.shape)


def solution(mesh):
    return jax.shard_map(
        on_device,
        mesh=mesh,
        in_specs=(P("sub", None, None, "grid", None), P("sub", "grid", None), P("sub", None)),
        out_specs=P("sub", None, None, "grid", None),
        check_vma=False,
    )
```

time: 936 us -> 164 us (0.18)
  waiting for transfers between devices: 336 us -> 18.8 us
  other arithmetic: 242 us -> 24.4 us
  local copies, waits for them, and re-layouts: 193 us -> 12.8 us
  matrix products: 129 us -> 0 us
  Pallas kernels: 0 us -> 101 us
  between operations: 14.4 us -> 0.09 us
    psum x8 -> x0, waiting for transfers between devices: 273 us -> none  [broadcast(): return lax.psum(jnp.where(mine, shard, jnp.zeros_like(shard)), axis)]
    another operation x40 -> x10, other arithmetic: 183 us -> 22.2 us  [the longest x3 5.88 us: ring_gather(): return jnp.stack(parts)]
    dot_general x25 -> x0, matrix products: 127 us -> none  [the longest x17 111 us: outer_product(): lax.dot_general(left, right, (((1,), (1,)), ((), ())), precision=precisio...]
    pallas_call x0 -> x3, Pallas kernels: none -> 101 us  [the longest x1 51.2 us: factor_pivots(): pl.pallas_call(functools.partial(pivot_kernel, grid_count), grid=(1,), in...]
    gather x8 -> x0, local copies, waits for them, and re-layouts: 98.9 us -> none  [the longest x4 46.1 us: select_rows(): picked = table[jnp.where(found, index, 0)]]
    all_to_all x1 -> x0, waiting for transfers between devices: 62.5 us -> none  [on_device(): lax.all_to_all(spread.astype(jnp.bfloat16), 'grid', split_axis=1, concat_...]
    select_n x24 -> x0, other arithmetic: 26.5 us -> none  [the longest x8 13.8 us: broadcast(): return lax.psum(jnp.where(mine, shard, jnp.zeros_like(shard)), axis)]
    reshape x2 -> x0, local copies, waits for them, and re-layouts: 21.6 us -> none  [the longest x1 12 us: on_device(): return result.reshape(front_entries.shape)]
  transfers between devices with their start and end apart: 27 -> 7, of which waited for: 9 -> 3; matrix products, arithmetic and copies ran while one was open for 33% -> 18% of each run, Pallas kernels for 0% -> 7%
where the time goes in v1:
time: 164 us; the launch traced here: 163 us
  Pallas kernels  101 us (62%)
  other arithmetic  24.4 us (15%)
  waiting for transfers between devices  18.8 us (11%)
  local copies, waits for them, and re-layouts  12.8 us (8%)
  starting transfers between devices  6.12 us (4%)
    pallas_call x1, Pallas kernels, factor_pivots(): pl.pallas_call(functools.partial(pivot_kernel, grid_count), grid=(1,), in...  51.2 us
    pallas_call x1, Pallas kernels, schur(): pl.pallas_call(functools.partial(schur_kernel, grid_count), grid=(front.s...  39.1 us
    ppermute x3, waiting for transfers between devices, ring_gather(): lax.ppermute(shard, 'grid', [((i + k) % count, i) for i in range(count)])  17 us
    pallas_call x1, Pallas kernels, expand(): pl.pallas_call(expand_kernel, grid=(PF // tile,), in_specs=[pl.BlockSpec(...  11 us
    unnamed x11, local copies, waits for them, and re-layouts  10.3 us
    another operation x3, other arithmetic, ring_gather(): return jnp.stack(parts)  5.88 us
    another operation x2, other arithmetic, on_device(): pivots = jnp.stack([held, sibling_swap(held)])  5.11 us
    ppermute x3, starting transfers between devices, ring_gather(): lax.ppermute(shard, 'grid', [((i + k) % count, i) for i in range(count)])  5.04 us
  transfers between devices with their start and end apart: 7, of which 3 were waited for; matrix products, arithmetic and copies ran while one was open for 18% of the time, Pallas kernels for 7%

profile of v1, /device:TPU:0, one launch (start us, length us, event | category | flops | bytes accessed | tf_op | source)
XLA Modules:
  0.0 163.4 jit_solution(17349224521820218275)
XLA Ops:
  0.0 3.0 %collective-permute-start.3 = (bf16[1024,256]{1,0:T(8,128)(2,1)}, bf16[1024,256]{1,0:T(8,128)(2,1)}, u32[]{:S(2)}, u32[]{:S(2)}) collective-permute-start(bf16[1024,256]{1,0:T(8,128)(2,1)} %bitcast.32), channel_id=1, source_target_pairs={{1,0},{0,1},{3,2},{2,3},{5,4},{4,5},{7,6},{6,7},{9,8},{8,9},{11,10... | collective-permute-start | bytes 1572872 | tf_op jit(solution)/shard_map/ppermute | solution.py:45
  3.0 5.2 %copy.5 = f32[1,12,128,1,1536]{4,2,3,1,0:T(8,128)S(1)} copy(f32[1,12,128,1,1536]{4,3,2,1,0:T(1,128)} %param.3) | data formatting | bytes 18874368
  8.2 0.0 copy-start
  8.2 3.7 %copy-done = f32[1,12,128,1,1536]{4,2,3,1,0:T(8,128)} copy-done((f32[1,12,128,1,1536]{4,2,3,1,0:T(8,128)}, f32[1,12,128,1,1536]{4,2,3,1,0:T(8,128)S(1)}, u32[]{:S(2)}) %copy-start) | copy-done | bytes 9437208
  11.9 0.1 slice.21
  12.0 1.5 fusion.1
  13.5 0.9 fusion.11
  14.5 0.0 collective-permute-start.5
  14.5 4.3 %bitcast_convert_fusion = bf16[1536,1536]{1,0:T(8,128)(2,1)S(1)} fusion(f32[1,12,128,1,1536]{4,2,3,1,0:T(8,128)} %copy-done), kind=kLoop, calls=%fused_computation.30 | loop fusion | flops 2359296 | bytes 14155776 | tf_op jit(solution)/shard_map/convert.1
  18.7 1.1 slice_bitcast_fusion.1
  19.8 0.0 copy-start.2
  19.8 0.0 copy-start.3
  19.8 2.0 %collective-permute-start = (bf16[1024,512]{1,0:T(8,128)(2,1)}, bf16[1024,512]{1,0:T(8,128)(2,1)}, u32[]{:S(2)}, u32[]{:S(2)}) collective-permute-start(bf16[1024,512]{1,0:T(8,128)(2,1)} %get-tuple-element.14), channel_id=1, source_target_pairs={{1,0},{0,1},{3,2},{2,3},{5,4},{4,5},{7,6},{6,7},{9,8},{8,9},{11,10... | collective-permute-start | bytes 3145736 | tf_op jit(solution)/shard_map/ppermute | solution.py:45
  21.9 1.3 slice_bitcast_fusion
  23.1 0.0 collective-permute-start.1
  23.2 0.0 collective-permute-done.3
  23.2 0.0 copy-done.2
  23.2 2.1 %pad_maximum_fusion.5 = bf16[2,1024,256]{2,1,0:T(8,128)(2,1)} fusion(bf16[1,1024,256]{2,1,0:T(8,128)(2,1)} %bitcast.9, bf16[1,1024,256]{2,1,0:T(8,128)(2,1)S(1)} %copy-done.2), kind=kLoop, calls=%fused_computation.8 | loop fusion | flops 524288 | bytes 2097152 | tf_op jit(solution)/shard_map/stack | solution.py:46
  25.3 0.5 collective-permute-start.4
  25.8 0.5 broadcast.134
  26.3 0.0 copy-done.3
  26.3 0.6 reduce.3
  26.9 2.7 %collective-permute-done.5 = bf16[528,512]{1,0:T(8,128)(2,1)S(1)} collective-permute-done((bf16[528,512]{1,0:T(8,128)(2,1)S(1)}, bf16[528,512]{1,0:T(8,128)(2,1)S(1)}, u32[]{:S(2)}, u32[]{:S(2)}) %collective-permute-start.5) | collective-permute-done | bytes 540704 | tf_op jit(solution)/shard_map/ppermute | solution.py:45
  29.6 0.0 copy-start.1
  29.6 0.8 copy-done.1
  30.4 2.3 %fusion.12 = (bf16[1,2,528,512]{3,2,1,0:T(8,128)(2,1)S(1)}, bf16[2,528,512]{2,1,0:T(8,128)(2,1)}) fusion(bf16[1,528,512]{2,1,0:T(8,128)(2,1)} %bitcast.31, bf16[1,528,512]{2,1,0:T(8,128)(2,1)} %get-tuple-element.17), kind=kLoop, calls=%fused_computation.34 | loop fusion | flops 540672 | bytes 3244032 | tf_op jit(solution)/shard_map/stack | solution.py:291
  32.8 0.0 collective-permute-start.6
  32.8 0.6 collective-permute-start.2
  33.4 0.6 pad_add_fusion.1.me_ref
  34.0 1.8 %collective-permute-done.2 = s32[1,2048]{1,0:T(1,128)S(1)} collective-permute-done((s32[1,2048]{1,0:T(1,128)S(1)}, s32[1,2048]{1,0:T(1,128)S(1)}, u32[]{:S(2)}, u32[]{:S(2)}) %collective-permute-start.2) | collective-permute-done | bytes 8224 | tf_op jit(solution)/shard_map/ppermute | solution.py:38
  35.8 0.6 pad_add_fusion.map_ref
  36.4 14.4 %collective-permute-done = bf16[1024,512]{1,0:T(8,128)(2,1)} collective-permute-done((bf16[1024,512]{1,0:T(8,128)(2,1)}, bf16[1024,512]{1,0:T(8,128)(2,1)}, u32[]{:S(2)}, u32[]{:S(2)}) %collective-permute-start) | collective-permute-done | bytes 1048608 | tf_op jit(solution)/shard_map/ppermute | solution.py:45
  50.8 2.8 %pad_maximum_fusion.1.left_ref = bf16[2,1024,512]{2,1,0:T(8,128)(2,1)} fusion(bf16[1,1024,512]{2,1,0:T(8,128)(2,1)} %bitcast.4, bf16[1,1024,512]{2,1,0:T(8,128)(2,1)S(1)} %get-tuple-element.13), kind=kLoop, calls=%fused_computation.1 | loop fusion | flops 1048576 | bytes 4194304 | tf_op jit(solution)/shard_map/stack | solution.py:46
  53.6 0.0 collective-permute-done.1
  53.6 2.7 %pad_maximum_fusion.2.right_ref = bf16[2,512,1024]{2,1,0:T(8,128)(2,1)} fusion(bf16[1,512,1024]{2,1,0:T(8,128)(2,1)} %bitcast.6, bf16[1,512,1024]{2,1,0:T(8,128)(2,1)S(1)} %get-tuple-element.11), kind=kLoop, calls=%fused_computation.2 | loop fusion | flops 1048576 | bytes 4194304 | tf_op jit(solution)/shard_map/stack | solution.py:294
  56.3 0.0 collective-permute-done.4
  56.3 3.1 %pad_maximum_fusion.3.rows_ref = bf16[2,2048,256]{2,1,0:T(8,128)(2,1)} fusion(bf16[1,2048,256]{2,1,0:T(8,128)(2,1)} %bitcast.12, bf16[1,2048,256]{2,1,0:T(8,128)(2,1)} %bitcast.10), kind=kLoop, calls=%fused_computation.3 | loop fusion | flops 1048576 | bytes 4194304 | tf_op jit(solution)/shard_map/stack | solution.py:278
  59.4 11.0 %expand.1.rows_ref = bf16[3072,512]{1,0:T(8,128)(2,1)} custom-call(s32[2,1,2048]{2,1,0:T(1,128)} %pad_add_fusion.map_ref, bf16[2,2048,256]{2,1,0:T(8,128)(2,1)} %pad_maximum_fusion.3.rows_ref), custom_call_target="tpu_custom_call" | custom-call | tf_op jit(solution)/shard_map/expand/pallas_call | solution.py:66
  70.3 0.0 collective-permute-done.6
  70.4 2.8 %pad_maximum_fusion.front_ref = bf16[2,2,528,512]{3,2,1,0:T(8,128)(2,1)} fusion(bf16[1,2,528,512]{3,2,1,0:T(8,128)(2,1)} %bitcast.16, bf16[1,2,528,512]{3,2,1,0:T(8,128)(2,1)S(1)} %get-tuple-element.15), kind=kLoop, calls=%fused_computation | loop fusion | flops 1081344 | bytes 4325376 | tf_op jit(solution)/shard_map/stack | solution.py:291
  73.1 51.2 %pivots.1 = (f32[1024,1024]{1,0:T(8,128)}, bf16[1024,1024]{1,0:T(8,128)(2,1)}, bf16[1024,1024]{1,0:T(8,128)(2,1)}) custom-call(s32[2]{0:T(128)} %pad_add_fusion.1.me_ref, bf16[2,2,528,512]{3,2,1,0:T(8,128)(2,1)} %pad_maximum_fusion.front_ref, bf16[3072,512]{1,0:T(8,128)(2,1)} %expand.1.rows_ref), custom_call_target="tpu_custom_call" | custom-call | flops 42949672960 | bytes 16777216 | tf_op jit(solution)/shard_map/pivots/pallas_call | solution.py:167
  124.3 39.1 %schur.1 = f32[18432,128]{1,0:T(8,128)} custom-call(s32[2]{0:T(128)} %pad_add_fusion.1.me_ref, f32[18432,128]{1,0:T(8,128)} %bitcast.30, bf16[2,1024,512]{2,1,0:T(8,128)(2,1)} %pad_maximum_fusion.1.left_ref, bf16[2,512,1024]{2,1,0:T(8,128)(2,1)} %pad_maximum_fusion.2.right_ref, bf16[3072,512]{1,0:T(8,128)(2,1)} %expand.1.rows_ref, ...), custom_call_target="tpu_custom_call" | custom-call | tf_op jit(solution)/shard_map/schur/pallas_call | solution.py:243
  (7 shorter events, 0.1 us)
Async XLA Ops:
  0.0 23.2 %collective-permute-start.3 = (bf16[1024,256]{1,0:T(8,128)(2,1)}, bf16[1024,256]{1,0:T(8,128)(2,1)}, u32[]{:S(2)}, u32[]{:S(2)}) collective-permute-start(bf16[1024,256]{1,0:T(8,128)(2,1)} %bitcast.32), channel_id=1, source_target_pairs={{1,0},{0,1},{3,2},{2,3},{5,4},{4,5},{7,6},{6,7},{9,8},{8,9},{11,10... | collective-permute-start | bytes 1572872 | tf_op jit(solution)/shard_map/ppermute | solution.py:45
  8.2 3.7 %copy-start = (f32[1,12,128,1,1536]{4,2,3,1,0:T(8,128)}, f32[1,12,128,1,1536]{4,2,3,1,0:T(8,128)S(1)}, u32[]{:S(2)}) copy-start(f32[1,12,128,1,1536]{4,2,3,1,0:T(8,128)S(1)} %copy.5) | copy-start | bytes 28311556
  14.5 15.1 %collective-permute-start.5 = (bf16[528,512]{1,0:T(8,128)(2,1)S(1)}, bf16[528,512]{1,0:T(8,128)(2,1)S(1)}, u32[]{:S(2)}, u32[]{:S(2)}) collective-permute-start(bf16[528,512]{1,0:T(8,128)(2,1)S(1)} %get-tuple-element.18), channel_id=1, source_target_pairs={{1,0},{0,1},{3,2},{2,3},{5,4},{4,5},{7,6},{6,7},{9,8},{8,9},{11,10... | collective-permute-start | bytes 1622024 | tf_op jit(solution)/shard_map/ppermute | solution.py:45
  19.8 3.3 %copy-start.2 = (bf16[1,1024,256]{2,1,0:T(8,128)(2,1)S(1)}, bf16[1,1024,256]{2,1,0:T(8,128)(2,1)}, u32[]{:S(2)}) copy-start(bf16[1,1024,256]{2,1,0:T(8,128)(2,1)} %param.4) | copy-start | bytes 1572868
  19.8 6.5 %copy-start.3 = (s32[1,2048]{1,0:T(1,128)S(1)}, s32[1,2048]{1,0:T(1,128)}, u32[]{:S(2)}) copy-start(s32[1,2048]{1,0:T(1,128)} %param.5) | copy-start | bytes 24580
  19.8 30.9 %collective-permute-start = (bf16[1024,512]{1,0:T(8,128)(2,1)}, bf16[1024,512]{1,0:T(8,128)(2,1)}, u32[]{:S(2)}, u32[]{:S(2)}) collective-permute-start(bf16[1024,512]{1,0:T(8,128)(2,1)} %get-tuple-element.14), channel_id=1, source_target_pairs={{1,0},{0,1},{3,2},{2,3},{5,4},{4,5},{7,6},{6,7},{9,8},{8,9},{11,10... | collective-permute-start | bytes 3145736 | tf_op jit(solution)/shard_map/ppermute | solution.py:45
  23.1 30.4 %collective-permute-start.1 = (bf16[512,1024]{1,0:T(8,128)(2,1)}, bf16[512,1024]{1,0:T(8,128)(2,1)}, u32[]{:S(2)}, u32[]{:S(2)}) collective-permute-start(bf16[512,1024]{1,0:T(8,128)(2,1)} %get-tuple-element.12), channel_id=1, source_target_pairs={{0,2},{2,0},{4,6},{6,4},{8,10},{10,8},{12,14},{14,12},{16,18},{18,... | collective-permute-start | bytes 3145736 | tf_op jit(solution)/shard_map/ppermute | solution.py:38
  25.3 31.0 %collective-permute-start.4 = (bf16[2048,256]{1,0:T(8,128)(2,1)}, bf16[2048,256]{1,0:T(8,128)(2,1)}, u32[]{:S(2)}, u32[]{:S(2)}) collective-permute-start(bf16[2048,256]{1,0:T(8,128)(2,1)} %bitcast.11), channel_id=1, source_target_pairs={{0,2},{2,0},{4,6},{6,4},{8,10},{10,8},{12,14},{14,12},{16,18},{18,... | collective-permute-start | bytes 3145736 | tf_op jit(solution)/shard_map/ppermute | solution.py:38
  29.6 0.8 copy-start.1
  32.8 37.6 %collective-permute-start.6 = (bf16[2,528,512]{2,1,0:T(8,128)(2,1)}, bf16[2,528,512]{2,1,0:T(8,128)(2,1)}, u32[]{:S(2)}, u32[]{:S(2)}) collective-permute-start(bf16[2,528,512]{2,1,0:T(8,128)(2,1)} %get-tuple-element.16), channel_id=1, source_target_pairs={{0,2},{2,0},{4,6},{6,4},{8,10},{10,8},{12,14},{14,12},{16,18},{18,... | collective-permute-start | bytes 3244040 | tf_op jit(solution)/shard_map/ppermute | solution.py:38
  32.8 3.0 %collective-permute-start.2 = (s32[1,2048]{1,0:T(1,128)S(1)}, s32[1,2048]{1,0:T(1,128)S(1)}, u32[]{:S(2)}, u32[]{:S(2)}) collective-permute-start(s32[1,2048]{1,0:T(1,128)S(1)} %bitcast.33), channel_id=1, source_target_pairs={{0,2},{2,0},{4,6},{6,4},{8,10},{10,8},{12,14},{14,12},{16,18},{18,... | collective-permute-start | bytes 24584 | tf_op jit(solution)/shard_map/ppermute | solution.py:38
